TPU v7x, 512 devices: a whole 4x4x16 slice. The times are simulated.
512 devices in a mesh: tm: 128 (over y, x_hi, z), col: 4 (over x_lo, core).
Axes of the slice: x: 4 (x_hi: 2, x_lo: 2; x = x_hi * 2 + x_lo), y: 4, z: 16, core: 2. Of those that a mesh axis runs over, the one named last changes fastest.
Arguments:
- frames: bfloat16 [384, 2, 96, 384], P('tm', None, 'col'), may hold values from -6 to 6
- up_kernel: bfloat16 [10368, 256], P(None, 'tm'), may hold values from -0.109375 to 0.109375
- mix_kernel: bfloat16 [6912, 256], P(None, 'tm'), may hold values from -0.078125 to 0.078125
- cotangent: bfloat16 [768, 2, 96, 256], P('tm', None, 'col'), may hold values from -6 to 6
Outputs:
- decoded: bfloat16 [768, 2, 96, 256], P('tm', None, 'col')
- frames_grad: bfloat16 [384, 2, 96, 384], P('tm', None, 'col')
All inputs are finite; a program needn't handle non-finite values.
Results may differ from a plain program's by a relative error of at most 0.005.
Values may be sent and summed in bfloat16 or wider, within the bound.
No kernel may reach another device: no remote copies, remote signals or barrier semaphores. Data moves between devices by JAX's collectives and lax.ppermute only.
A program may use at most 64 MiB of HBM per device.

v0:
```python
import jax
import jax.numpy as jnp
from jax import lax
from jax.sharding import PartitionSpec as P


def with_halo(block, sides, width):
    for axis, dim in sides:
        count = lax.axis_size(axis)
        forward = [(i, i + 1) for i in range(count - 1)]
        backward = [(target, source) for source, target in forward]
        low = lax.ppermute(
            lax.slice_in_dim(block, block.shape[dim] - width, None, axis=dim), axis, forward
        )
        high = lax.ppermute(lax.slice_in_dim(block, 0, width, axis=dim), axis, backward)
        block = jnp.concatenate([low, block, high], axis=dim)
    return block


def from_behind(array, axis, by):
    devices = lax.axis_size(axis)
    pairs = [(i, i + by) for i in range(devices) if 0 <= i + by < devices]
    return lax.ppermute(array, axis, pairs)


def widen(field):
    return with_halo(field, (("col", 2),), 1)


def from_previous(field):
    return from_behind(field, "tm", 1)


def from_next(field):
    return from_behind(field, "tm", -1)


def forward_pass(kernel, produce):
    return produce(lax.all_gather(kernel, "tm", axis=1, tiled=True), jnp.int32(0))


def backward_pass(kernel, combine, initial):
    return combine(initial, lax.all_gather(kernel, "tm", axis=1, tiled=True), jnp.int32(0))


def pad_rows(field):
    return jnp.pad(field, ((0, 0), (1, 1), (0, 0), (0, 0)))


def window(padded, first, count, row_low, col_low, height, width):
    part = padded[first : first + count, row_low : row_low + height, col_low : col_low + width]
    return part.reshape(-1, part.shape[-1])


def transposed(rows, matrix):
    return lax.dot_general(
        rows, matrix, (((1,), (1,)), ((), ())), preferred_element_type=jnp.float32
    )


def shards(frames, up_kernel, mix_kernel, cotangent):
    frame_count, height, width, in_channels = frames.shape
    out_channels = mix_kernel.shape[0] // 27
    count = 2 * frame_count
    block = count * height * width
    widened = widen(frames)
    earlier = from_previous(widened[-1:])
    extended = pad_rows(jnp.concatenate((earlier, widened), axis=0))
    rows_in = extended.shape[0] - 1

    def up_columns(piece, start):
        taps = piece.reshape(3, 3, 3, in_channels, piece.shape[1])
        even = jnp.zeros((rows_in * height * width, piece.shape[1]), jnp.float32)
        odd = even
        for tap_h in range(3):
            for tap_w in range(3):
                current = window(extended, 1, rows_in, tap_h, tap_w, height, width)
                prior = window(extended, 0, rows_in, tap_h, tap_w, height, width)
                even = even + jnp.dot(
                    current, taps[0, tap_h, tap_w], preferred_element_type=jnp.float32
                )
                even = even + jnp.dot(
                    prior, taps[2, tap_h, tap_w], preferred_element_type=jnp.float32
                )
                odd = odd + jnp.dot(
                    current, taps[1, tap_h, tap_w], preferred_element_type=jnp.float32
                )
        stacked = jnp.stack(
            (even.reshape(rows_in, height * width, -1), odd.reshape(rows_in, height * width, -1)),
            axis=1,
        )
        return stacked.reshape(-1, piece.shape[1])

    before_all = forward_pass(up_kernel, up_columns).reshape(
        2 * rows_in, height, width, out_channels
    )
    hidden = jax.nn.silu(before_all).astype(jnp.bfloat16)
    earlier_hidden = from_previous(hidden[-2:])
    hidden_pad = pad_rows(widen(jnp.concatenate((earlier_hidden, hidden), axis=0)))
    cot_pad = pad_rows(widen(jnp.concatenate((cotangent, from_next(cotangent[:2])), axis=0)))

    def mix_forward(piece, start):
        taps = piece.reshape(3, 3, 3, out_channels, piece.shape[1])
        total = jnp.zeros((block, piece.shape[1]), jnp.float32)
        for tap_t in range(3):
            for tap_h in range(3):
                for tap_w in range(3):
                    total = total + jnp.dot(
                        window(hidden_pad, tap_t, count, tap_h, tap_w, height, width),
                        taps[tap_t, tap_h, tap_w],
                        preferred_element_type=jnp.float32,
                    )
        return total

    def mix_backward(piece):
        taps = piece.reshape(3, 3, 3, out_channels, piece.shape[1])
        total = jnp.zeros((block, out_channels), jnp.float32)
        for tap_t in range(3):
            for tap_h in range(3):
                for tap_w in range(3):
                    total = total + transposed(
                        window(cot_pad, 2 - tap_t, count, 2 - tap_h, 2 - tap_w, height, width),
                        taps[tap_t, tap_h, tap_w],
                    )
        return total

    empty = jnp.zeros((block, out_channels), jnp.float32)
    decoded_flat = forward_pass(mix_kernel, mix_forward)

    def accumulate(total, piece, start):
        return mix_backward(piece)

    hidden_grad = backward_pass(mix_kernel, accumulate, empty)
    flat_before = before_all.reshape(block, out_channels)
    sigma = jax.nn.sigmoid(flat_before)
    before_grad = (hidden_grad * sigma * (1.0 + flat_before * (1.0 - sigma))).astype(jnp.bfloat16)
    before_grad = before_grad.reshape(count, height, width, out_channels)
    grad_pad = pad_rows(widen(jnp.concatenate((before_grad, from_next(before_grad[:1])), axis=0)))
    evens = grad_pad[0::2]
    odds = grad_pad[1::2]

    def up_backward(total, piece, start):
        taps = piece.reshape(3, 3, 3, in_channels, piece.shape[1])
        for tap_h in range(3):
            for tap_w in range(3):
                total = total + transposed(
                    window(evens, 0, frame_count, 2 - tap_h, 2 - tap_w, height, width),
                    taps[0, tap_h, tap_w],
                )
                total = total + transposed(
                    window(odds, 0, frame_count, 2 - tap_h, 2 - tap_w, height, width),
                    taps[1, tap_h, tap_w],
                )
                total = total + transposed(
                    window(evens, 1, frame_count, 2 - tap_h, 2 - tap_w, height, width),
                    taps[2, tap_h, tap_w],
                )
        return total

    grad_start = jnp.zeros((frame_count * height * width, in_channels), jnp.float32)
    grad_total = backward_pass(up_kernel, up_backward, grad_start)
    decoded = decoded_flat.astype(jnp.bfloat16).reshape(count, height, width, out_channels)
    frames_grad = grad_total.astype(jnp.bfloat16).reshape(frame_count, height, width, in_channels)
    return (decoded, frames_grad)


def solution(mesh):
    placed = (P("tm", None, "col", None), P(None, "tm"), P(None, "tm"), P("tm", None, "col", None))
    return jax.shard_map(
        shards,
        mesh=mesh,
        in_specs=placed,
        out_specs=(P("tm", None, "col", None), P("tm", None, "col", None)),
        check_vma=False,
    )
```

profile of v0, /device:TPU:1, one launch (start us, length us, event | category | flops | bytes accessed | tf_op | source)
XLA Modules:
  0.0 542.3 jit_solution(755618982540305264)
XLA Ops:
  9.5 8.8 %collective-permute-start.1 = (bf16[3,2,1,384]{3,2,1,0:T(2,128)(2,1)S(1)}, bf16[3,2,1,384]{3,2,1,0:T(2,128)(2,1)S(1)}, u32[]{:S(2)}, u32[]{:S(2)}) collective-permute-start(bf16[3,2,1,384]{3,2,1,0:T(2,128)(2,1)S(1)} %get-tuple-element.114), channel_id=1, source_target_pairs={{1,0},{2,1},{3,2},{5,4},{6,5},{7,6},{9,8},{10,9},{11,10},{13,12},{... | collective-permute-start | bytes 13832 | tf_op jit(solution)/shard_map/ppermute | solution.py:15
  18.3 1.9 collective-permute-start
  21.0 1.3 collective-permute-start.6
  22.3 0.9 constant_dynamic-update-slice_fusion.1
  24.0 4.0 collective-permute-start.2
  28.0 1.7 pad_maximum_fusion.5
  29.8 1.0 maximum_maximum_fusion.1
  30.8 3.0 collective-permute-start.8
  33.8 2.6 collective-permute-start.7
  36.4 1.2 pad_slice_fusion
  37.8 1.1 pad_maximum_fusion.2
  38.9 1.5 fusion.45
  40.5 188.4 %all-gather.7.cloned.1.call-done = bf16[128,2,6912]{2,1,0:T(2,128)(2,1)} async-done(((bf16[1,2,6912]{2,1,0:T(2,128)(2,1)}), bf16[128,2,6912]{2,1,0:T(2,128)(2,1)}) %all-gather.7.cloned.1.call-update) | async-done | bytes 3538960 | tf_op jit(solution)/shard_map/all_gather | solution.py:39
  228.9 8.3 %reshape.429 = bf16[256,6912]{1,0:T(8,128)(2,1)} reshape(bf16[128,2,6912]{2,1,0:T(2,128)(2,1)} %all-gather.7.cloned.1.call-done) | data formatting | bytes 7077888
  237.1 5.0 copy.18
  242.2 1.2 fusion.44
  243.4 1.2 fusion.43
  244.6 1.2 fusion.41
  245.8 1.1 fusion.40
  246.9 1.2 fusion.38
  248.1 1.1 convolution_add_fusion.21
  249.2 1.2 convolution_add_fusion.20
  250.4 1.2 convolution_add_fusion.19
  255.8 0.9 convolution_add_fusion.1
  256.8 200.9 %all-gather.5.cloned.1.call-done = bf16[128,2,10368]{2,1,0:T(2,128)(2,1)} async-done(((bf16[1,2,10368]{2,1,0:T(2,128)(2,1)}), bf16[128,2,10368]{2,1,0:T(2,128)(2,1)}) %all-gather.5.cloned.1.call-update) | async-done | bytes 5308432 | tf_op jit(solution)/shard_map/all_gather | solution.py:39
  457.7 7.9 %reshape.427 = bf16[256,10368]{1,0:T(8,128)(2,1)} reshape(bf16[128,2,10368]{2,1,0:T(2,128)(2,1)} %all-gather.5.cloned.1.call-done) | data formatting | bytes 10616832
  465.6 8.0 %copy.15 = bf16[10368,256]{1,0:T(8,128)(2,1)} copy(bf16[10368,256]{0,1:T(8,128)(2,1)} %bitcast.565) | data formatting | bytes 10616832
  473.7 1.3 fusion.30
  475.0 1.7 fusion.27
  476.7 1.2 fusion.32
  477.9 1.2 fusion.31
  479.1 1.2 fusion.29
  480.3 1.2 fusion.28
  481.5 1.2 convolution_add_fusion.78
  482.7 1.2 convolution_add_fusion.93
  483.9 1.2 convolution_add_fusion.92
  485.1 1.2 convolution_add_fusion.77
  486.3 1.2 convolution_add_fusion.91
  491.3 1.3 collective-permute-start.9
  492.6 3.3 collective-permute-done.9
  495.9 12.7 %collective-permute-start.11 = (bf16[7,2,1,256]{3,2,1,0:T(2,128)(2,1)S(1)}, bf16[7,2,1,256]{3,2,1,0:T(2,128)(2,1)S(1)}, u32[]{:S(2)}, u32[]{:S(2)}) collective-permute-start(bf16[7,2,1,256]{3,2,1,0:T(2,128)(2,1)S(1)} %get-tuple-element.110), channel_id=1, source_target_pairs={{1,0},{2,1},{3,2},{5,4},{6,5},{7,6},{9,8},{10,9},{11,10},{13,12},{... | collective-permute-start | bytes 21512 | tf_op jit(solution)/shard_map/ppermute | solution.py:15
  508.7 2.1 collective-permute-start.10
  510.9 2.9 collective-permute-start.3
  520.1 0.9 fusion.9
  521.0 2.7 collective-permute-start.4
  523.7 1.9 collective-permute-start.5
  525.7 3.1 collective-permute-done.5
  534.6 0.9 fusion.7
  (189 shorter events, 23.5 us)
Async XLA Ops:
  7.2 221.7 %all-gather.7.cloned.1.call-start = ((), (), s32[]{:S(2)}) async-start(), calls=%async_computation.1 | async-start | bytes 3566592 | tf_op jit(solution)/shard_map/all_gather | solution.py:39
  7.9 449.8 %all-gather.5.cloned.1.call-start = ((), (), s32[]{:S(2)}) async-start(), calls=%async_computation | async-start | bytes 5349888 | tf_op jit(solution)/shard_map/all_gather | solution.py:39
  9.5 13.7 %collective-permute-start.1 = (bf16[3,2,1,384]{3,2,1,0:T(2,128)(2,1)S(1)}, bf16[3,2,1,384]{3,2,1,0:T(2,128)(2,1)S(1)}, u32[]{:S(2)}, u32[]{:S(2)}) collective-permute-start(bf16[3,2,1,384]{3,2,1,0:T(2,128)(2,1)S(1)} %get-tuple-element.114), channel_id=1, source_target_pairs={{1,0},{2,1},{3,2},{5,4},{6,5},{7,6},{9,8},{10,9},{11,10},{13,12},{... | collective-permute-start | bytes 13832 | tf_op jit(solution)/shard_map/ppermute | solution.py:15
  18.3 5.0 collective-permute-start
  21.0 9.8 %collective-permute-start.6 = (bf16[2,2,24,256]{3,2,1,0:T(8,128)(2,1)S(1)}, bf16[2,2,24,256]{3,2,1,0:T(8,128)(2,1)S(1)}, u32[]{:S(2)}, u32[]{:S(2)}) collective-permute-start(bf16[2,2,24,256]{3,2,1,0:T(8,128)(2,1)S(1)} %slice.702), channel_id=1, source_target_pairs={{4,0},{8,4},{12,8},{16,12},{20,16},{24,20},{28,24},{32,28},{36,32}... | collective-permute-start | bytes 147464 | tf_op jit(solution)/shard_map/ppermute | solution.py:23
  24.0 5.7 %collective-permute-start.2 = (bf16[1,2,26,384]{3,2,1,0:T(8,128)(2,1)S(1)}, bf16[1,2,26,384]{3,2,1,0:T(8,128)(2,1)S(1)}, u32[]{:S(2)}, u32[]{:S(2)}) collective-permute-start(bf16[1,2,26,384]{3,2,1,0:T(8,128)(2,1)S(1)} %pad_maximum_fusion.7), channel_id=1, source_target_pairs={{0,4},{4,8},{8,12},{12,16},{16,20},{20,24},{24,28},{28,32},{32,36}... | collective-permute-start | bytes 119816 | tf_op jit(solution)/shard_map/ppermute | solution.py:23
  30.8 6.8 %collective-permute-start.8 = (bf16[8,2,1,256]{3,2,1,0:T(2,128)(2,1)S(1)}, bf16[8,2,1,256]{3,2,1,0:T(2,128)(2,1)S(1)}, u32[]{:S(2)}, u32[]{:S(2)}) collective-permute-start(bf16[8,2,1,256]{3,2,1,0:T(2,128)(2,1)S(1)} %get-tuple-element.87), channel_id=1, source_target_pairs={{1,0},{2,1},{3,2},{5,4},{6,5},{7,6},{9,8},{10,9},{11,10},{13,12},{... | collective-permute-start | bytes 24584 | tf_op jit(solution)/shard_map/ppermute | solution.py:15
  33.8 3.9 collective-permute-start.7
  242.1 9.5 %copy-start.12 = (bf16[6,2,24,256]{3,2,1,0:T(8,128)(2,1)S(1)}, bf16[6,2,24,256]{3,2,1,0:T(8,128)(2,1)}, u32[]{:S(2)}) copy-start(bf16[6,2,24,256]{3,2,1,0:T(8,128)(2,1)} %get-tuple-element.85) | copy-start | bytes 442372
  242.1 9.7 %copy-start.27 = (bf16[6,2,24,256]{3,2,1,0:T(8,128)(2,1)S(1)}, bf16[6,2,24,256]{3,2,1,0:T(8,128)(2,1)}, u32[]{:S(2)}) copy-start(bf16[6,2,24,256]{3,2,1,0:T(8,128)(2,1)} %get-tuple-element.16) | copy-start | bytes 442372
  242.1 10.0 %copy-start.26 = (bf16[6,2,24,256]{3,2,1,0:T(8,128)(2,1)S(1)}, bf16[6,2,24,256]{3,2,1,0:T(8,128)(2,1)}, u32[]{:S(2)}) copy-start(bf16[6,2,24,256]{3,2,1,0:T(8,128)(2,1)} %get-tuple-element.15) | copy-start | bytes 442372
  242.1 10.2 %copy-start.25 = (bf16[6,2,24,256]{3,2,1,0:T(8,128)(2,1)S(1)}, bf16[6,2,24,256]{3,2,1,0:T(8,128)(2,1)}, u32[]{:S(2)}) copy-start(bf16[6,2,24,256]{3,2,1,0:T(8,128)(2,1)} %get-tuple-element.14) | copy-start | bytes 442372
  242.1 10.5 %copy-start.24 = (bf16[6,2,24,256]{3,2,1,0:T(8,128)(2,1)S(1)}, bf16[6,2,24,256]{3,2,1,0:T(8,128)(2,1)}, u32[]{:S(2)}) copy-start(bf16[6,2,24,256]{3,2,1,0:T(8,128)(2,1)} %get-tuple-element.13) | copy-start | bytes 442372
  242.2 10.7 %copy-start.23 = (bf16[6,2,24,256]{3,2,1,0:T(8,128)(2,1)S(1)}, bf16[6,2,24,256]{3,2,1,0:T(8,128)(2,1)}, u32[]{:S(2)}) copy-start(bf16[6,2,24,256]{3,2,1,0:T(8,128)(2,1)} %get-tuple-element.12) | copy-start | bytes 442372
  243.4 9.7 %copy-start.22 = (bf16[6,2,24,256]{3,2,1,0:T(8,128)(2,1)S(1)}, bf16[6,2,24,256]{3,2,1,0:T(8,128)(2,1)}, u32[]{:S(2)}) copy-start(bf16[6,2,24,256]{3,2,1,0:T(8,128)(2,1)} %get-tuple-element.11) | copy-start | bytes 442372
  244.6 8.8 %copy-start.13 = (bf16[6,2,24,256]{3,2,1,0:T(8,128)(2,1)S(1)}, bf16[6,2,24,256]{3,2,1,0:T(8,128)(2,1)}, u32[]{:S(2)}) copy-start(bf16[6,2,24,256]{3,2,1,0:T(8,128)(2,1)} %get-tuple-element.81) | copy-start | bytes 442372
  246.9 6.7 %copy-start.11 = (bf16[6,2,24,256]{3,2,1,0:T(8,128)(2,1)S(1)}, bf16[6,2,24,256]{3,2,1,0:T(8,128)(2,1)}, u32[]{:S(2)}) copy-start(bf16[6,2,24,256]{3,2,1,0:T(8,128)(2,1)} %get-tuple-element.84) | copy-start | bytes 442372
  249.2 4.6 copy-start.21
  250.4 3.7 copy-start.20
  251.6 2.8 copy-start.19
  251.6 3.0 copy-start.18
  251.9 3.0 copy-start.17
  252.1 3.0 copy-start.16
  252.4 2.9 copy-start.10
  252.9 2.7 copy-start.9
  253.1 2.7 copy-start.15
  473.6 13.9 %copy-start = (bf16[10368,256]{1,0:T(8,128)(2,1)S(1)}, bf16[10368,256]{1,0:T(8,128)(2,1)}, u32[]{:S(2)}) copy-start(bf16[10368,256]{1,0:T(8,128)(2,1)} %copy.15) | copy-start | bytes 15925252
  473.6 13.9 %copy-start.6 = (bf16[3,2,24,384]{3,2,1,0:T(8,128)(2,1)S(1)}, bf16[3,2,24,384]{3,2,1,0:T(8,128)(2,1)}, u32[]{:S(2)}) copy-start(bf16[3,2,24,384]{3,2,1,0:T(8,128)(2,1)} %get-tuple-element.98) | copy-start | bytes 331780
  473.6 14.1 %copy-start.32 = (bf16[3,2,24,384]{3,2,1,0:T(8,128)(2,1)S(1)}, bf16[3,2,24,384]{3,2,1,0:T(8,128)(2,1)}, u32[]{:S(2)}) copy-start(bf16[3,2,24,384]{3,2,1,0:T(8,128)(2,1)} %get-tuple-element.99) | copy-start | bytes 331780
  473.6 14.3 %copy-start.8 = (bf16[3,2,24,384]{3,2,1,0:T(8,128)(2,1)S(1)}, bf16[3,2,24,384]{3,2,1,0:T(8,128)(2,1)}, u32[]{:S(2)}) copy-start(bf16[3,2,24,384]{3,2,1,0:T(8,128)(2,1)} %get-tuple-element.112) | copy-start | bytes 331780
  473.6 14.6 %copy-start.1 = (bf16[3,2,24,384]{3,2,1,0:T(8,128)(2,1)S(1)}, bf16[3,2,24,384]{3,2,1,0:T(8,128)(2,1)}, u32[]{:S(2)}) copy-start(bf16[3,2,24,384]{3,2,1,0:T(8,128)(2,1)} %param.4) | copy-start | bytes 331780
  473.6 14.8 %copy-start.31 = (bf16[3,2,24,384]{3,2,1,0:T(8,128)(2,1)S(1)}, bf16[3,2,24,384]{3,2,1,0:T(8,128)(2,1)}, u32[]{:S(2)}) copy-start(bf16[3,2,24,384]{3,2,1,0:T(8,128)(2,1)} %get-tuple-element.106) | copy-start | bytes 331780
  473.6 15.0 %copy-start.7 = (bf16[3,2,24,384]{3,2,1,0:T(8,128)(2,1)S(1)}, bf16[3,2,24,384]{3,2,1,0:T(8,128)(2,1)}, u32[]{:S(2)}) copy-start(bf16[3,2,24,384]{3,2,1,0:T(8,128)(2,1)} %get-tuple-element.111) | copy-start | bytes 331780
  473.6 15.2 %copy-start.3 = (bf16[3,2,24,384]{3,2,1,0:T(8,128)(2,1)S(1)}, bf16[3,2,24,384]{3,2,1,0:T(8,128)(2,1)}, u32[]{:S(2)}) copy-start(bf16[3,2,24,384]{3,2,1,0:T(8,128)(2,1)} %get-tuple-element.100) | copy-start | bytes 331780
  477.9 11.5 %copy-start.5 = (bf16[3,2,24,384]{3,2,1,0:T(8,128)(2,1)S(1)}, bf16[3,2,24,384]{3,2,1,0:T(8,128)(2,1)}, u32[]{:S(2)}) copy-start(bf16[3,2,24,384]{3,2,1,0:T(8,128)(2,1)} %get-tuple-element.102) | copy-start | bytes 331780
  479.1 10.5 %copy-start.30 = (bf16[3,2,24,384]{3,2,1,0:T(8,128)(2,1)S(1)}, bf16[3,2,24,384]{3,2,1,0:T(8,128)(2,1)}, u32[]{:S(2)}) copy-start(bf16[3,2,24,384]{3,2,1,0:T(8,128)(2,1)} %get-tuple-element.101) | copy-start | bytes 331780
  481.5 8.5 %copy-start.4 = (bf16[3,2,24,384]{3,2,1,0:T(8,128)(2,1)S(1)}, bf16[3,2,24,384]{3,2,1,0:T(8,128)(2,1)}, u32[]{:S(2)}) copy-start(bf16[3,2,24,384]{3,2,1,0:T(8,128)(2,1)} %get-tuple-element.104) | copy-start | bytes 331780
  482.7 7.5 %copy-start.29 = (bf16[3,2,24,384]{3,2,1,0:T(8,128)(2,1)S(1)}, bf16[3,2,24,384]{3,2,1,0:T(8,128)(2,1)}, u32[]{:S(2)}) copy-start(bf16[3,2,24,384]{3,2,1,0:T(8,128)(2,1)} %get-tuple-element.103) | copy-start | bytes 331780
  485.1 5.5 %copy-start.28 = (bf16[3,2,24,384]{3,2,1,0:T(8,128)(2,1)S(1)}, bf16[3,2,24,384]{3,2,1,0:T(8,128)(2,1)}, u32[]{:S(2)}) copy-start(bf16[3,2,24,384]{3,2,1,0:T(8,128)(2,1)} %get-tuple-element.94) | copy-start | bytes 331780
  488.0 3.1 copy-start.2
  488.0 3.1 copy-start.14
  491.3 4.6 collective-permute-start.9
  495.9 17.9 %collective-permute-start.11 = (bf16[7,2,1,256]{3,2,1,0:T(2,128)(2,1)S(1)}, bf16[7,2,1,256]{3,2,1,0:T(2,128)(2,1)S(1)}, u32[]{:S(2)}, u32[]{:S(2)}) collective-permute-start(bf16[7,2,1,256]{3,2,1,0:T(2,128)(2,1)S(1)} %get-tuple-element.110), channel_id=1, source_target_pairs={{1,0},{2,1},{3,2},{5,4},{6,5},{7,6},{9,8},{10,9},{11,10},{13,12},{... | collective-permute-start | bytes 21512 | tf_op jit(solution)/shard_map/ppermute | solution.py:15
  508.7 5.1 collective-permute-start.10
  510.9 10.1 %collective-permute-start.3 = (bf16[2,2,24,256]{3,2,1,0:T(8,128)(2,1)S(1)}, bf16[2,2,24,256]{3,2,1,0:T(8,128)(2,1)S(1)}, u32[]{:S(2)}, u32[]{:S(2)}) collective-permute-start(bf16[2,2,24,256]{3,2,1,0:T(8,128)(2,1)S(1)} %slice.794), channel_id=1, source_target_pairs={{0,4},{4,8},{8,12},{12,16},{16,20},{20,24},{24,28},{28,32},{32,36}... | collective-permute-start | bytes 147464 | tf_op jit(solution)/shard_map/ppermute | solution.py:23
  521.0 4.7 collective-permute-start.4
  523.7 5.1 collective-permute-start.5
Sparse Core Ops, SparseCore 0:
  12.5 216.3 all-gather.6
  233.4 224.2 all-gather.4
where the time goes:
time: 544 us; the launch traced here: 542 us
  waiting for transfers between devices  397 us (73%)
  starting transfers between devices  45.2 us (8%)
  matrix products  43.6 us (8%)
  local copies, waits for them, and re-layouts  35.3 us (6%)
  between operations  15.6 us (3%)
  other arithmetic  5.54 us (1%)
    all_gather x2, waiting for transfers between devices, forward_pass(): lax.all_gather(kernel, 'tm', axis=1, tiled=True)  389 us
    unnamed x71, local copies, waits for them, and re-layouts  30.2 us
    ppermute x4, starting transfers between devices, with_halo(): lax.ppermute(lax.slice_in_dim(block, 0, width, axis=dim), axis, backward)  26.4 us
    dot_general x54, matrix products, transposed(): lax.dot_general(rows, matrix, (((1,), (1,)), ((), ())), preferred_element...  21 us
  transfers between devices with their start and end apart: 14, of which 4 were waited for; matrix products, arithmetic and copies ran while one was open for 8% of the time, Pallas kernels for 0%

commit v1 on v0

--- a/solution.py
+++ b/solution.py
@@ -36,7 +36,13 @@
 
 
 def forward_pass(kernel, produce):
-    return produce(lax.all_gather(kernel, "tm", axis=1, tiled=True), jnp.int32(0))
+    return produce(
+        jnp.concatenate(
+            lax.all_to_all(jnp.stack([kernel for _ in range(lax.axis_size("tm"))]), "tm", 0, 0),
+            axis=1,
+        ),
+        jnp.int32(0),
+    )
 
 
 def backward_pass(kernel, combine, initial):

time: 544 us -> 953 us (1.75)
  blocking collectives: 0 us -> 179 us
  local copies, waits for them, and re-layouts: 35.3 us -> 185 us
  waiting for transfers between devices: 397 us -> 449 us
  starting transfers between devices: 45.2 us -> 59.9 us
    ppermute x4, waiting for transfers between devices: 3.28 us -> 220 us  [from_behind(): return lax.ppermute(array, axis, pairs)]
    all_to_all x0 -> x1, blocking collectives: none -> 179 us  [forward_pass(): lax.all_to_all(jnp.stack([kernel for _ in range(lax.axis_size('tm'))]), '...]
    all_gather x2, waiting for transfers between devices: 389 us -> 225 us  [backward_pass(): lax.all_gather(kernel, 'tm', axis=1, tiled=True)]
    slice x0 -> x58, local copies, waits for them, and re-layouts: none -> 114 us  [the longest x29 45.5 us: mix_forward(): taps[tap_t, tap_h, tap_w]]
    another operation x0 -> x4, local copies, waits for them, and re-layouts: none -> 37.3 us  [the longest x1 17.3 us: up_columns(): taps = piece.reshape(3, 3, 3, in_channels, piece.shape[1])]
    all_to_all x0 -> x1, starting transfers between devices: none -> 14.4 us  [forward_pass(): lax.all_to_all(jnp.stack([kernel for _ in range(lax.axis_size('tm'))]), '...]
    unnamed x71 -> x171, local copies, waits for them, and re-layouts: 30.2 us -> 30.3 us
  transfers between devices with their start and end apart: 14 -> 15, of which waited for: 4 -> 5; matrix products, arithmetic and copies ran while one was open for 8% -> 12% of each run, Pallas kernels for 0% -> 0%
where the time goes in v1:
time: 953 us; the launch traced here: 943 us
  waiting for transfers between devices  449 us (47%)
  local copies, waits for them, and re-layouts  185 us (19%)
  blocking collectives  179 us (19%)
  starting transfers between devices  59.9 us (6%)
  matrix products  48.4 us (5%)
  between operations  16.6 us (2%)
    all_gather x2, waiting for transfers between devices, backward_pass(): lax.all_gather(kernel, 'tm', axis=1, tiled=True)  225 us
    ppermute x4, waiting for transfers between devices, from_behind(): return lax.ppermute(array, axis, pairs)  220 us
    all_to_all x1, blocking collectives, forward_pass(): lax.all_to_all(jnp.stack([kernel for _ in range(lax.axis_size('tm'))]), '...  179 us
    slice x29, local copies, waits for them, and re-layouts, mix_forward(): taps[tap_t, tap_h, tap_w]  45.5 us
    unnamed x171, local copies, waits for them, and re-layouts  30.3 us
    slice x10, local copies, waits for them, and re-layouts, up_columns(): taps[2, tap_h, tap_w]  29.3 us
    ppermute x4, starting transfers between devices, with_halo(): lax.ppermute(lax.slice_in_dim(block, 0, width, axis=dim), axis, backward)  24.7 us
    dot_general x54, matrix products, transposed(): lax.dot_general(rows, matrix, (((1,), (1,)), ((), ())), preferred_element...  23.7 us
  transfers between devices with their start and end apart: 15, of which 5 were waited for; matrix products, arithmetic and copies ran while one was open for 12% of the time, Pallas kernels for 0%

profile of v1, /device:TPU:1, one launch (start us, length us, event | category | flops | bytes accessed | tf_op | source)
XLA Modules:
  0.0 942.5 jit_solution(14279617166301909395)
XLA Ops:
  7.2 2.6 stack.8
  9.8 179.3 %all_to_all.10 = bf16[128,6912,2]{1,2,0:T(2,128)(2,1)} all-to-all(bf16[128,6912,2]{1,2,0:T(2,128)(2,1)S(1)} %stack.8), channel_id=1, replica_groups=mesh['tm'=128,'col'=4] {'tm'}, dimensions={0} | all-to-all | bytes 7077888 | tf_op jit(solution)/shard_map/all_to_all | solution.py:41
  189.1 5.1 stack.6
  194.2 14.4 %all-to-all-start = ((bf16[128,10368,2]{1,2,0:T(2,128)(2,1)}), bf16[128,10368,2]{1,2,0:T(2,128)(2,1)}, u32[]{:S(2)}, u32[]{:S(2)}) async-start(bf16[128,10368,2]{1,2,0:T(2,128)(2,1)} %stack.6), calls=%async_computation | async-start | bytes 10616832 | tf_op jit(solution)/shard_map/all_to_all | solution.py:41
  210.1 3.3 collective-permute-start.1
  213.5 2.2 collective-permute-start
  217.1 4.0 collective-permute-start.2
  221.9 213.3 %collective-permute-done.2 = bf16[1,2,26,384]{3,2,1,0:T(8,128)(2,1)S(1)} collective-permute-done((bf16[1,2,26,384]{3,2,1,0:T(8,128)(2,1)S(1)}, bf16[1,2,26,384]{3,2,1,0:T(8,128)(2,1)S(1)}, u32[]{:S(2)}, u32[]{:S(2)}) %collective-permute-start.2) | collective-permute-done | bytes 39968 | tf_op jit(solution)/shard_map/ppermute | solution.py:23
  435.2 6.5 collective-permute-done.6
  441.7 7.9 collective-permute-start.8
  449.6 2.1 collective-permute-start.7
  455.9 26.3 %all-gather.5.cloned.1.call-done = bf16[128,2,6912]{2,1,0:T(2,128)(2,1)} async-done(((bf16[1,2,6912]{2,1,0:T(2,128)(2,1)}), bf16[128,2,6912]{2,1,0:T(2,128)(2,1)}) %all-gather.5.cloned.1.call-update) | async-done | bytes 3538960 | tf_op jit(solution)/shard_map/all_gather | solution.py:49
  482.2 8.7 reshape.437
  490.9 5.0 copy.127
  510.6 198.7 %all-gather.7.cloned.1.call-done = bf16[128,2,10368]{2,1,0:T(2,128)(2,1)} async-done(((bf16[1,2,10368]{2,1,0:T(2,128)(2,1)}), bf16[128,2,10368]{2,1,0:T(2,128)(2,1)}) %all-gather.7.cloned.1.call-update) | async-done | bytes 5308432 | tf_op jit(solution)/shard_map/all_gather | solution.py:49
  709.3 7.9 reshape.439
  717.2 8.0 copy.128
  725.2 12.3 %reshape_reshape.11 = bf16[3,3,3,256,256]{3,2,1,0,4:T(4,128)(2,1)} reshape(bf16[6912,128,2]{0,2,1:T(2,128)(2,1)} %bitcast.629) | data formatting | bytes 7077888 | tf_op jit(solution)/shard_map/reshape;reshape | solution.py:109
  737.5 8.9 fusion.101
  746.4 17.3 %reshape_reshape.9 = bf16[3,3,3,384,256]{3,2,1,0,4:T(4,128)(2,1)} reshape(bf16[10368,128,2]{0,2,1:T(2,128)(2,1)} %bitcast.1) | data formatting | bytes 10616832 | tf_op jit(solution)/shard_map/reshape;reshape | solution.py:78
  763.8 12.9 %fusion.99 = (bf16[1,1,1,384,256]{3,2,1,0,4:T(2,128)(2,1)}, bf16[1,1,1,384,256]{3,2,1,0,4:T(2,128)(2,1)}, bf16[1,1,1,384,256]{3,2,1,0,4:T(2,128)(2,1)}, bf16[1,1...) fusion(bf16[3,3,3,384,256]{3,2,1,0,4:T(4,128)(2,1)} %reshape_re, ...), kind=kLoop, calls=%fused_computation.300 | loop fusion | bytes 7471104 | tf_op jit(solution)/shard_map/slice | solution.py:89
  776.7 6.0 fusion.100
  782.6 1.8 copy.95
  784.5 1.8 copy.93
  786.3 1.8 copy.89
  795.4 1.8 copy.96
  799.0 1.8 copy.82
  800.8 1.8 copy.78
  802.7 1.8 copy.71
  804.5 1.8 fusion.37
  806.3 1.8 fusion.58
  808.2 1.8 copy.72
  811.8 1.8 copy.74
  817.3 1.8 copy.77
  822.8 1.8 copy.81
  824.6 1.8 copy.83
  826.4 1.8 copy.84
  828.3 1.8 copy.85
  830.1 1.8 copy.86
  833.7 1.8 copy.88
  855.0 4.5 fusion.102
  859.6 1.8 copy.114
  891.9 11.6 %collective-permute-start.11 = (bf16[7,2,1,256]{3,2,1,0:T(2,128)(2,1)S(1)}, bf16[7,2,1,256]{3,2,1,0:T(2,128)(2,1)S(1)}, u32[]{:S(2)}, u32[]{:S(2)}) collective-permute-start(bf16[7,2,1,256]{3,2,1,0:T(2,128)(2,1)S(1)} %get-tuple-element.164), channel_id=1, source_target_pairs={{1,0},{2,1},{3,2},{5,4},{6,5},{7,6},{9,8},{10,9},{11,10},{13,12},{... | collective-permute-start | bytes 21512 | tf_op jit(solution)/shard_map/ppermute | solution.py:15
  903.4 2.1 collective-permute-start.10
  905.7 4.7 collective-permute-start.3
  920.5 2.8 collective-permute-start.4
  923.3 1.9 collective-permute-start.5
  925.3 3.1 collective-permute-done.5
  (355 shorter events, 107.7 us)
Async XLA Ops:
  7.2 181.9 %copy-start.80 = (bf16[10368,2]{0,1:T(2,128)(2,1)S(1)}, bf16[10368,2]{0,1:T(2,128)(2,1)}, u32[]{:S(2)}) copy-start(bf16[10368,2]{0,1:T(2,128)(2,1)} %param.5) | copy-start | bytes 124420
  194.2 15.9 %copy-start = (bf16[3,2,24,384]{3,2,1,0:T(8,128)(2,1)S(1)}, bf16[3,2,24,384]{3,2,1,0:T(8,128)(2,1)}, u32[]{:S(2)}) copy-start(bf16[3,2,24,384]{3,2,1,0:T(8,128)(2,1)} %param.4) | copy-start | bytes 331780
  194.2 21.6 %copy-start.19 = (bf16[6,2,24,256]{3,2,1,0:T(8,128)(2,1)S(1)}, bf16[6,2,24,256]{3,2,1,0:T(8,128)(2,1)}, u32[]{:S(2)}) copy-start(bf16[6,2,24,256]{3,2,1,0:T(8,128)(2,1)} %param.7) | copy-start | bytes 442372
  194.2 552.3 %all-to-all-start = ((bf16[128,10368,2]{1,2,0:T(2,128)(2,1)}), bf16[128,10368,2]{1,2,0:T(2,128)(2,1)}, u32[]{:S(2)}, u32[]{:S(2)}) async-start(bf16[128,10368,2]{1,2,0:T(2,128)(2,1)} %stack.6), calls=%async_computation | async-start | bytes 10616832 | tf_op jit(solution)/shard_map/all_to_all | solution.py:41
  208.6 273.6 %all-gather.5.cloned.1.call-start = ((), (), s32[]{:S(2)}) async-start(), calls=%async_computation.2 | async-start | bytes 3566592 | tf_op jit(solution)/shard_map/all_gather | solution.py:49
  209.3 499.9 %all-gather.7.cloned.1.call-start = ((), (), s32[]{:S(2)}) async-start(), calls=%async_computation.3 | async-start | bytes 5349888 | tf_op jit(solution)/shard_map/all_gather | solution.py:49
  210.1 6.9 collective-permute-start.1
  213.5 3.6 collective-permute-start
  215.7 226.0 %collective-permute-start.6 = (bf16[2,2,24,256]{3,2,1,0:T(8,128)(2,1)S(1)}, bf16[2,2,24,256]{3,2,1,0:T(8,128)(2,1)S(1)}, u32[]{:S(2)}, u32[]{:S(2)}) collective-permute-start(bf16[2,2,24,256]{3,2,1,0:T(8,128)(2,1)S(1)} %slice.810), channel_id=1, source_target_pairs={{4,0},{8,4},{12,8},{16,12},{20,16},{24,20},{28,24},{32,28},{36,32}... | collective-permute-start | bytes 147464 | tf_op jit(solution)/shard_map/ppermute | solution.py:23
  217.1 218.0 %collective-permute-start.2 = (bf16[1,2,26,384]{3,2,1,0:T(8,128)(2,1)S(1)}, bf16[1,2,26,384]{3,2,1,0:T(8,128)(2,1)S(1)}, u32[]{:S(2)}, u32[]{:S(2)}) collective-permute-start(bf16[1,2,26,384]{3,2,1,0:T(8,128)(2,1)S(1)} %pad_maximum_fusion.7), channel_id=1, source_target_pairs={{0,4},{4,8},{8,12},{12,16},{16,20},{20,24},{24,28},{28,32},{32,36}... | collective-permute-start | bytes 119816 | tf_op jit(solution)/shard_map/ppermute | solution.py:23
  441.7 11.2 %collective-permute-start.8 = (bf16[8,2,1,256]{3,2,1,0:T(2,128)(2,1)S(1)}, bf16[8,2,1,256]{3,2,1,0:T(2,128)(2,1)S(1)}, u32[]{:S(2)}, u32[]{:S(2)}) collective-permute-start(bf16[8,2,1,256]{3,2,1,0:T(2,128)(2,1)S(1)} %get-tuple-element.141), channel_id=1, source_target_pairs={{1,0},{2,1},{3,2},{5,4},{6,5},{7,6},{9,8},{10,9},{11,10},{13,12},{... | collective-permute-start | bytes 24584 | tf_op jit(solution)/shard_map/ppermute | solution.py:15
  449.6 3.4 collective-permute-start.7
  495.9 10.7 %copy-start.50 = (bf16[6,2,24,256]{3,2,1,0:T(8,128)(2,1)S(1)}, bf16[6,2,24,256]{3,2,1,0:T(8,128)(2,1)}, u32[]{:S(2)}) copy-start(bf16[6,2,24,256]{3,2,1,0:T(8,128)(2,1)} %get-tuple-element.66) | copy-start | bytes 442372
  835.6 12.6 %copy-start.33 = (bf16[1,1,1,384,256]{4,3,2,1,0:T(8,128)(2,1)S(1)}, bf16[1,1,1,384,256]{4,3,2,1,0:T(8,128)(2,1)}, u32[]{:S(2)}) copy-start(bf16[1,1,1,384,256]{4,3,2,1,0:T(8,128)(2,1)} %copy.76) | copy-start | bytes 589828
  835.6 12.6 %copy-start.79 = (bf16[3,2,24,384]{3,2,1,0:T(8,128)(2,1)S(1)}, bf16[3,2,24,384]{3,2,1,0:T(8,128)(2,1)}, u32[]{:S(2)}) copy-start(bf16[3,2,24,384]{3,2,1,0:T(8,128)(2,1)} %get-tuple-element.153) | copy-start | bytes 331780
  835.6 12.8 %copy-start.18 = (bf16[3,2,24,384]{3,2,1,0:T(8,128)(2,1)S(1)}, bf16[3,2,24,384]{3,2,1,0:T(8,128)(2,1)}, u32[]{:S(2)}) copy-start(bf16[3,2,24,384]{3,2,1,0:T(8,128)(2,1)} %get-tuple-element.166) | copy-start | bytes 331780
  835.6 12.8 %copy-start.34 = (bf16[1,1,1,384,256]{4,3,2,1,0:T(8,128)(2,1)S(1)}, bf16[1,1,1,384,256]{4,3,2,1,0:T(8,128)(2,1)}, u32[]{:S(2)}) copy-start(bf16[1,1,1,384,256]{4,3,2,1,0:T(8,128)(2,1)} %copy.77) | copy-start | bytes 589828
  835.6 13.1 %copy-start.1 = (bf16[3,2,24,384]{3,2,1,0:T(8,128)(2,1)S(1)}, bf16[3,2,24,384]{3,2,1,0:T(8,128)(2,1)}, u32[]{:S(2)}) copy-start(bf16[3,2,24,384]{3,2,1,0:T(8,128)(2,1)} %param.4) | copy-start | bytes 331780
  835.6 13.0 %copy-start.32 = (bf16[1,1,1,384,256]{4,3,2,1,0:T(8,128)(2,1)S(1)}, bf16[1,1,1,384,256]{4,3,2,1,0:T(8,128)(2,1)}, u32[]{:S(2)}) copy-start(bf16[1,1,1,384,256]{4,3,2,1,0:T(8,128)(2,1)} %copy.79) | copy-start | bytes 589828
  835.6 13.2 %copy-start.31 = (bf16[1,1,1,384,256]{4,3,2,1,0:T(8,128)(2,1)S(1)}, bf16[1,1,1,384,256]{4,3,2,1,0:T(8,128)(2,1)}, u32[]{:S(2)}) copy-start(bf16[1,1,1,384,256]{4,3,2,1,0:T(8,128)(2,1)} %copy.80) | copy-start | bytes 589828
  835.6 13.2 %copy-start.78 = (bf16[3,2,24,384]{3,2,1,0:T(8,128)(2,1)S(1)}, bf16[3,2,24,384]{3,2,1,0:T(8,128)(2,1)}, u32[]{:S(2)}) copy-start(bf16[3,2,24,384]{3,2,1,0:T(8,128)(2,1)} %get-tuple-element.160) | copy-start | bytes 331780
  835.6 13.4 %copy-start.17 = (bf16[3,2,24,384]{3,2,1,0:T(8,128)(2,1)S(1)}, bf16[3,2,24,384]{3,2,1,0:T(8,128)(2,1)}, u32[]{:S(2)}) copy-start(bf16[3,2,24,384]{3,2,1,0:T(8,128)(2,1)} %get-tuple-element.165) | copy-start | bytes 331780
  835.6 13.4 %copy-start.30 = (bf16[1,1,1,384,256]{4,3,2,1,0:T(8,128)(2,1)S(1)}, bf16[1,1,1,384,256]{4,3,2,1,0:T(8,128)(2,1)}, u32[]{:S(2)}) copy-start(bf16[1,1,1,384,256]{4,3,2,1,0:T(8,128)(2,1)} %copy.81) | copy-start | bytes 589828
  835.7 13.6 %copy-start.14 = (bf16[3,2,24,384]{3,2,1,0:T(8,128)(2,1)S(1)}, bf16[3,2,24,384]{3,2,1,0:T(8,128)(2,1)}, u32[]{:S(2)}) copy-start(bf16[3,2,24,384]{3,2,1,0:T(8,128)(2,1)} %get-tuple-element.154) | copy-start | bytes 331780
  835.7 13.6 %copy-start.29 = (bf16[1,1,1,384,256]{4,3,2,1,0:T(8,128)(2,1)S(1)}, bf16[1,1,1,384,256]{4,3,2,1,0:T(8,128)(2,1)}, u32[]{:S(2)}) copy-start(bf16[1,1,1,384,256]{4,3,2,1,0:T(8,128)(2,1)} %copy.83) | copy-start | bytes 589828
  835.7 13.8 %copy-start.23 = (bf16[1,1,1,384,256]{4,3,2,1,0:T(8,128)(2,1)S(1)}, bf16[1,1,1,384,256]{4,3,2,1,0:T(8,128)(2,1)}, u32[]{:S(2)}) copy-start(bf16[1,1,1,384,256]{4,3,2,1,0:T(8,128)(2,1)} %copy.92) | copy-start | bytes 589828
  835.7 14.0 %copy-start.22 = (bf16[1,1,1,384,256]{4,3,2,1,0:T(8,128)(2,1)S(1)}, bf16[1,1,1,384,256]{4,3,2,1,0:T(8,128)(2,1)}, u32[]{:S(2)}) copy-start(bf16[1,1,1,384,256]{4,3,2,1,0:T(8,128)(2,1)} %copy.94) | copy-start | bytes 589828
  837.0 12.9 %copy-start.16 = (bf16[3,2,24,384]{3,2,1,0:T(8,128)(2,1)S(1)}, bf16[3,2,24,384]{3,2,1,0:T(8,128)(2,1)}, u32[]{:S(2)}) copy-start(bf16[3,2,24,384]{3,2,1,0:T(8,128)(2,1)} %get-tuple-element.156) | copy-start | bytes 331780
  837.0 12.9 %copy-start.21 = (bf16[1,1,1,384,256]{4,3,2,1,0:T(8,128)(2,1)S(1)}, bf16[1,1,1,384,256]{4,3,2,1,0:T(8,128)(2,1)}, u32[]{:S(2)}) copy-start(bf16[1,1,1,384,256]{4,3,2,1,0:T(8,128)(2,1)} %copy.96) | copy-start | bytes 589828
  838.3 11.9 %copy-start.28 = (bf16[1,1,1,384,256]{4,3,2,1,0:T(8,128)(2,1)S(1)}, bf16[1,1,1,384,256]{4,3,2,1,0:T(8,128)(2,1)}, u32[]{:S(2)}) copy-start(bf16[1,1,1,384,256]{4,3,2,1,0:T(8,128)(2,1)} %copy.84) | copy-start | bytes 589828
  838.3 11.9 %copy-start.77 = (bf16[3,2,24,384]{3,2,1,0:T(8,128)(2,1)S(1)}, bf16[3,2,24,384]{3,2,1,0:T(8,128)(2,1)}, u32[]{:S(2)}) copy-start(bf16[3,2,24,384]{3,2,1,0:T(8,128)(2,1)} %get-tuple-element.155) | copy-start | bytes 331780
  839.5 10.9 %copy-start.27 = (bf16[1,1,1,384,256]{4,3,2,1,0:T(8,128)(2,1)S(1)}, bf16[1,1,1,384,256]{4,3,2,1,0:T(8,128)(2,1)}, u32[]{:S(2)}) copy-start(bf16[1,1,1,384,256]{4,3,2,1,0:T(8,128)(2,1)} %copy.85) | copy-start | bytes 589828
  853.6 36.5 %copy-start.13 = (bf16[1,1,1,256,256]{3,2,1,0,4:T(2,128)(2,1)S(1)}, bf16[1,1,1,256,256]{3,2,1,0,4:T(2,128)(2,1)}, u32[]{:S(2)}) copy-start(bf16[1,1,1,256,256]{3,2,1,0,4:T(2,128)(2,1)} %get-tuple-element.35) | copy-start | bytes 393220
  853.6 37.3 %copy-start.12 = (bf16[1,1,1,256,256]{3,2,1,0,4:T(2,128)(2,1)S(1)}, bf16[1,1,1,256,256]{3,2,1,0,4:T(2,128)(2,1)}, u32[]{:S(2)}) copy-start(bf16[1,1,1,256,256]{3,2,1,0,4:T(2,128)(2,1)} %get-tuple-element.34) | copy-start | bytes 393220
  853.6 38.2 %collective-permute-start.9 = (bf16[1,2,24,256]{3,2,1,0:T(8,128)(2,1)}, bf16[1,2,24,256]{3,2,1,0:T(8,128)(2,1)S(1)}, u32[]{:S(2)}, u32[]{:S(2)}) collective-permute-start(bf16[1,2,24,256]{3,2,1,0:T(8,128)(2,1)} %bitcast.167), channel_id=1, source_target_pairs={{4,0},{8,4},{12,8},{16,12},{20,16},{24,20},{28,24},{32,28},{36,32}... | collective-permute-start | bytes 73736 | tf_op jit(solution)/shard_map/ppermute | solution.py:23
  859.6 31.5 %copy-start.11 = (bf16[1,1,1,256,256]{3,2,1,0,4:T(2,128)(2,1)S(1)}, bf16[1,1,1,256,256]{3,2,1,0,4:T(2,128)(2,1)}, u32[]{:S(2)}) copy-start(bf16[1,1,1,256,256]{3,2,1,0,4:T(2,128)(2,1)} %get-tuple-element.33) | copy-start | bytes 393220
  859.6 31.6 %copy-start.10 = (bf16[1,1,1,256,256]{3,2,1,0,4:T(2,128)(2,1)S(1)}, bf16[1,1,1,256,256]{3,2,1,0,4:T(2,128)(2,1)}, u32[]{:S(2)}) copy-start(bf16[1,1,1,256,256]{3,2,1,0,4:T(2,128)(2,1)} %get-tuple-element.32) | copy-start | bytes 393220
  859.6 31.8 %copy-start.9 = (bf16[1,1,1,256,256]{3,2,1,0,4:T(2,128)(2,1)S(1)}, bf16[1,1,1,256,256]{3,2,1,0,4:T(2,128)(2,1)}, u32[]{:S(2)}) copy-start(bf16[1,1,1,256,256]{3,2,1,0,4:T(2,128)(2,1)} %get-tuple-element.31) | copy-start | bytes 393220
  859.6 31.9 %copy-start.8 = (bf16[1,1,1,256,256]{3,2,1,0,4:T(2,128)(2,1)S(1)}, bf16[1,1,1,256,256]{3,2,1,0,4:T(2,128)(2,1)}, u32[]{:S(2)}) copy-start(bf16[1,1,1,256,256]{3,2,1,0,4:T(2,128)(2,1)} %get-tuple-element.30) | copy-start | bytes 393220
  859.6 32.0 %copy-start.7 = (bf16[1,1,1,256,256]{3,2,1,0,4:T(2,128)(2,1)S(1)}, bf16[1,1,1,256,256]{3,2,1,0,4:T(2,128)(2,1)}, u32[]{:S(2)}) copy-start(bf16[1,1,1,256,256]{3,2,1,0,4:T(2,128)(2,1)} %get-tuple-element.29) | copy-start | bytes 393220
  859.6 32.2 %copy-start.5 = (bf16[288,256]{1,0:T(8,128)(2,1)S(1)}, bf16[288,256]{1,0:T(8,128)(2,1)}, u32[]{:S(2)}) copy-start(bf16[288,256]{1,0:T(8,128)(2,1)} %copy-done.4) | copy-start | bytes 442372
  861.5 44.1 %copy-start.3 = (f32[3,2,48,256]{3,2,1,0:T(8,128)S(1)}, f32[3,2,48,256]{3,2,1,0:T(8,128)}, u32[]{:S(2)}) copy-start(f32[3,2,48,256]{3,2,1,0:T(8,128)} %copy-done.2) | copy-start | bytes 884740
  871.6 42.7 %slice-start = ((s8[5308416]{0:T(1024)(128)(4,1)}), s8[1114112]{0:T(1024)(128)(4,1)S(1)}, s32[]{:S(2)}) async-start(s8[5308416]{0:T(1024)(128)(4,1)} %bitcast.575), calls=%async_computation.4 | async-start | bytes 2228224
  891.9 18.6 %collective-permute-start.11 = (bf16[7,2,1,256]{3,2,1,0:T(2,128)(2,1)S(1)}, bf16[7,2,1,256]{3,2,1,0:T(2,128)(2,1)S(1)}, u32[]{:S(2)}, u32[]{:S(2)}) collective-permute-start(bf16[7,2,1,256]{3,2,1,0:T(2,128)(2,1)S(1)} %get-tuple-element.164), channel_id=1, source_target_pairs={{1,0},{2,1},{3,2},{5,4},{6,5},{7,6},{9,8},{10,9},{11,10},{13,12},{... | collective-permute-start | bytes 21512 | tf_op jit(solution)/shard_map/ppermute | solution.py:15
  903.4 7.0 collective-permute-start.10
  905.7 14.7 %collective-permute-start.3 = (bf16[2,2,24,256]{3,2,1,0:T(8,128)(2,1)S(1)}, bf16[2,2,24,256]{3,2,1,0:T(8,128)(2,1)S(1)}, u32[]{:S(2)}, u32[]{:S(2)}) collective-permute-start(bf16[2,2,24,256]{3,2,1,0:T(8,128)(2,1)S(1)} %slice.956), channel_id=1, source_target_pairs={{0,4},{4,8},{8,12},{12,16},{16,20},{20,24},{24,28},{28,32},{32,36}... | collective-permute-start | bytes 147464 | tf_op jit(solution)/shard_map/ppermute | solution.py:23
  920.5 4.8 collective-permute-start.4
  923.3 5.1 collective-permute-start.5
  (50 other events, 252.1 us)
Sparse Core Ops, SparseCore 0:
  213.9 268.2 all-gather.4
  486.7 222.5 all-gather.6
